TPU v7x, 32 devices: a whole 2x2x4 slice. The times are simulated.
32 devices in a mesh: lat: 4 (over z), lon: 8 (over y, x, core).
Axes of the slice: x: 2, y: 2, z: 4, core: 2. Of those that a mesh axis runs over, the one named last changes fastest.
Arguments:
- background: bfloat16 [32768, 384], P(('lat', 'lon')), may hold values from -6 to 6
- increment: bfloat16 [32768, 384], P(('lat', 'lon')), may hold values from -6 to 6
- coefficients: bfloat16 [384, 4352], replicated, may hold values from -0.3125 to 0.3125
- departures: bfloat16 [128, 128, 4352], P(('lat', 'lon')), may hold values from -6 to 6
- bias_pred: float32 [128, 128, 8], P(('lat', 'lon')), may hold values from -6 to 6
- beta_incr: float32 [8, 4352], replicated, may hold values from -2 to 2
- obs_weight: float32 [4352], replicated, may hold values from 0.1 to 1
- obs_count: int32 [128], P(('lat', 'lon')), may hold values from 1 to 128
- col_index: int32 [128, 128], P(('lat', 'lon')), may hold values from 0 to 32767, as said below
Outputs:
- radiance: bfloat16 [128, 128, 4352], P(('lat', 'lon'))
- column_grad: bfloat16 [32768, 384], P(('lat', 'lon'))
- bias_grad: float32 [4352, 8], P(('lat', 'lon'))
Inputs may be any that keep to these rules, and one draw needn't show every extreme that they name: `col_index`: column c is owned by the block of 1024 columns c // 1024. Among the 512 slots of the blocks of one device, at most 24 name columns of any one owner, and some owner is named by exactly 24 slots of every device.
All inputs are finite; a program needn't handle non-finite values.
Results may differ from a plain program's by a relative error of at most 0.005.
Values may be sent and summed in bfloat16 or wider, within the bound.
A program may use at most 128 MiB of HBM per device.

v0:
```python
import jax
import jax.numpy as jnp
from jax import lax
from jax.sharding import PartitionSpec as P


def route_ids(requests):
    return lax.all_to_all(requests, ("lat", "lon"), split_axis=0, concat_axis=0, tiled=True)


def route_profiles(payload):
    return lax.all_to_all(payload, ("lat", "lon"), split_axis=0, concat_axis=0, tiled=True)


def route_adjoint(payload):
    return lax.all_to_all(payload, ("lat", "lon"), split_axis=0, concat_axis=0, tiled=True)


def shards(
    background,
    increment,
    coefficients,
    departures,
    bias_pred,
    beta_incr,
    obs_weight,
    obs_count,
    col_index,
):
    lat_count = lax.axis_size("lat")
    lon_count = lax.axis_size("lon")
    devices = lat_count * lon_count
    column_count, profile_len = background.shape
    block_count, block_len = col_index.shape
    channels = coefficients.shape[1]
    npredictors = bias_pred.shape[2]
    slot_count = block_count * block_len
    capacity = 3 * slot_count // (2 * devices)
    scaling = 1.0 / jnp.sqrt(jnp.float32(slot_count * devices))
    columns = col_index.reshape(slot_count)
    owners = columns // column_count
    local_cols = columns % column_count
    owner_table = (owners[:, None] == jnp.arange(devices, dtype=jnp.int32)[None, :]).astype(
        jnp.int32
    )
    bucket_rank = jnp.sum(jnp.cumsum(owner_table, axis=0) * owner_table, axis=1) - 1
    position = owners * capacity + bucket_rank
    requests = jnp.zeros((devices * capacity,), jnp.int32).at[position].set(local_cols)
    wanted = route_ids(requests.reshape(devices, capacity)).reshape(devices * capacity)
    base_rows = background[wanted]
    step_rows = increment[wanted]
    owner_jacobian = 1.0 + 0.5 * jnp.tanh(base_rows.astype(jnp.float32))
    formed_rows = (step_rows.astype(jnp.float32) * owner_jacobian).astype(jnp.bfloat16)
    arrived = route_profiles(formed_rows.reshape(devices, capacity, profile_len))
    predictor = arrived.reshape(devices * capacity, profile_len)[position]
    flat_pred = bias_pred.reshape(slot_count, npredictors)
    slot_pos = jnp.arange(block_len, dtype=jnp.int32)
    present = (slot_pos[None, :] < obs_count[:, None]).reshape(slot_count, 1)
    radiance_f = jnp.dot(predictor, coefficients, preferred_element_type=jnp.float32)
    radiance_f = radiance_f + jnp.dot(flat_pred, beta_incr, precision=lax.Precision.HIGHEST)
    radiance_f = jnp.where(present, radiance_f, jnp.float32(0.0))
    radiance = radiance_f.astype(jnp.bfloat16).reshape(block_count, block_len, channels)
    observed = departures.reshape(slot_count, channels).astype(jnp.float32)
    misfit = jnp.where(present, obs_weight[None, :] * (radiance_f - observed), jnp.float32(0.0))
    pulled = lax.dot_general(
        misfit.astype(jnp.bfloat16),
        coefficients,
        (((1,), (1,)), ((), ())),
        preferred_element_type=jnp.float32,
    )
    outgoing = jnp.zeros((devices * capacity, profile_len), jnp.float32).at[position].set(pulled)
    returned = route_adjoint(outgoing.reshape(devices, capacity, profile_len))
    returned = returned.reshape(devices * capacity, profile_len) * owner_jacobian
    gradient = jnp.zeros((column_count, profile_len), jnp.float32).at[wanted].add(returned)
    column_grad = gradient.astype(jnp.bfloat16)
    local_bias = (
        lax.dot_general(
            misfit, flat_pred, (((0,), (0,)), ((), ())), precision=lax.Precision.HIGHEST
        )
        * scaling
    )
    bias_grad = lax.psum_scatter(local_bias, ("lat", "lon"), scatter_dimension=0, tiled=True)
    return (radiance, column_grad, bias_grad)


def solution(mesh):
    return jax.shard_map(
        shards,
        mesh=mesh,
        in_specs=(
            P(("lat", "lon"), None),
            P(("lat", "lon"), None),
            P(),
            P(("lat", "lon"), None, None),
            P(("lat", "lon"), None, None),
            P(),
            P(),
            P(("lat", "lon")),
            P(("lat", "lon"), None),
        ),
        out_specs=(P(("lat", "lon"), None, None), P(("lat", "lon"), None), P(("lat", "lon"), None)),
        check_vma=False,
    )
```

profile of v0, /device:TPU:0, one launch (start us, length us, event | category | flops | bytes accessed | tf_op | source)
XLA Modules:
  0.0 246.5 jit_solution(12728389772487381901)
XLA Ops:
  7.2 0.0 copy-start
  7.2 0.8 add_select_fusion.2
  8.0 0.9 add_select_fusion.1
  8.9 1.2 reduce-window.6
  10.1 0.2 slice_reduce_fusion
  10.3 0.1 fusion.17
  10.4 0.7 compare_select_fusion.1
  11.1 2.4 scatter_custom_fusion
  13.6 0.1 all_to_all.12
  13.7 14.3 %all_to_all.19 = s32[32,1,24]{2,1,0:T(1,128)S(1)} all-to-all(s32[32,1,24]{2,1,0:T(1,128)S(1)} %bitcast.73), channel_id=1, replica_groups=mesh['lat'=4,'lon'=8] {'lat','lon'}, dimensions={0} | all-to-all | bytes 6144 | tf_op jit(solution)/shard_map/all_to_all | solution.py:8
  28.0 0.5 broadcast.224
  28.5 0.7 reduce.7
  29.2 0.1 reshape.215
  29.3 4.3 %gather_fusion.1 = bf16[768,384]{1,0:T(8,128)(2,1)} fusion(bf16[1024,384]{1,0:T(8,128)(2,1)} %param.9, s32[1024]{0:T(1024)S(1)} %pad_clamp_fusion.1), kind=kCustom, calls=%fused_computation.1 | custom fusion | bytes 1182720 | tf_op jit(solution)/shard_map/gather | solution.py:50
  33.7 0.0 copy-start.5
  33.7 4.4 %gather_fusion = bf16[768,384]{1,0:T(8,128)(2,1)} fusion(bf16[1024,384]{1,0:T(8,128)(2,1)} %param.10, s32[1024]{0:T(1024)S(1)} %pad_clamp_fusion.1), kind=kCustom, calls=%fused_computation | custom fusion | bytes 1182720 | tf_op jit(solution)/shard_map/gather | solution.py:51
  38.0 2.3 multiply_convert_fusion
  40.4 3.5 %all-to-all-start.1 = ((bf16[32,24,384]{2,1,0:T(8,128)(2,1)}), bf16[32,24,384]{2,1,0:T(8,128)(2,1)}, u32[]{:S(2)}, u32[]{:S(2)}) async-start(bf16[32,24,384]{2,1,0:T(8,128)(2,1)} %bitcast.72), calls=%async_computation.1 | async-start | bytes 1179648 | tf_op jit(solution)/shard_map/all_to_all | solution.py:12
  43.9 0.0 copy-done.5
  43.9 0.1 fusion.26
  44.0 16.5 %all-to-all-done.1 = bf16[32,24,384]{2,1,0:T(8,128)(2,1)} async-done(((bf16[32,24,384]{2,1,0:T(8,128)(2,1)}), bf16[32,24,384]{2,1,0:T(8,128)(2,1)}, u32[]{:S(2)}, u32[]{:S(2)}) %all-to-all-start.1) | async-done | bytes 589856 | tf_op jit(solution)/shard_map/all_to_all | solution.py:12
  60.5 3.6 %gather_fusion.2 = bf16[512,384]{1,0:T(8,128)(2,1)} fusion(bf16[768,384]{1,0:T(8,128)(2,1)} %bitcast.8, s32[1024]{0:T(1024)S(1)} %pad_clamp_fusion), kind=kCustom, calls=%fused_computation.2 | custom fusion | bytes 788480 | tf_op jit(solution)/shard_map/gather | solution.py:55
  64.1 0.0 copy-done
  64.1 0.0 copy-start.2
  64.1 0.0 copy-start.3
  64.1 0.0 slice-start
  64.1 3.6 %fusion.32 = f32[512,4352]{1,0:T(8,128)S(1)} fusion(bf16[512,384]{1,0:T(8,128)(2,1)} %gather_fusion.2, bf16[384,4352]{1,0:T(8,128)(2,1)S(1)} %copy-done), kind=kOutput, calls=%fused_computation.71 | convolution fusion | flops 1711276032 | bytes 12648448 | tf_op jit(solution)/shard_map/dot_general | solution.py:59
  67.7 0.0 copy-done.2
  67.7 0.0 copy-done.3
  67.7 0.0 slice-start.1
  67.7 0.0 copy-start.4
  67.7 9.2 %fusion.31 = (bf16[512,4352]{1,0:T(8,128)(2,1)}, f32[512,4352]{1,0:T(8,128)S(1)}) fusion(f32[512,4352]{1,0:T(8,128)S(1)} %fusion.32, f32[8,4352]{1,0:T(8,128)S(1)} %copy-done.2, f32[4,128,8]{1,2,0:T(8,128)S(1)} %copy-done.3, pred[512]{0:T(512)(128)(4,1)S(1)} %fusion.26), kind=kOutput, calls=%fused_computation.70 | convolution fusion | flops 220594176 | bytes 22438400 | tf_op jit(solution)/shard_map/dot_general | solution.py:60
  76.9 0.0 copy-start.1
  76.9 3.4 %copy-done.1 = f32[512,4352]{1,0:T(8,128)} copy-done((f32[512,4352]{1,0:T(8,128)}, f32[512,4352]{1,0:T(8,128)S(1)}, u32[]{:S(2)}) %copy-start.1) | copy-done | bytes 8912920
  80.4 0.0 slice-done
  80.4 0.0 slice-done.1
  80.4 0.0 copy-done.4
  80.4 3.4 %fusion.4 = f32[512,384]{1,0:T(8,128)} fusion(bf16[384,4352]{1,0:T(8,128)(2,1)S(1)} %copy-done, f32[512,4352]{1,0:T(8,128)S(1)} %get-tuple-element.6, bf16[512,4352]{1,0:T(8,128)(2,1)S(1)} %bitcast.70, f32[4352]{0:T(1024)S(1)} %copy-done.4, pred[512]{0:T(512)(128)(4,1)S(1)} %fusion.26), kind=kOutput, calls=%fused_computation.12 | convolution fusion | flops 1722417152 | bytes 17516032 | tf_op jit(solution)/shard_map/dot_general | solution.py:65
  83.8 3.9 %scatter_custom_fusion.1 = f32[768,384]{1,0:T(8,128)} fusion(s32[512]{0:T(512)S(1)} %bitcast.77, f32[512,384]{1,0:T(8,128)} %fusion.4, f32[]{:T(128)} %constant.50.clone.1), kind=kCustom, calls=%fused_computation.24 | custom fusion | bytes 1180160 | tf_op jit(solution)/shard_map/scatter | solution.py:71
  87.6 3.4 %all-to-all-start.2 = ((f32[32,24,384]{2,1,0:T(8,128)}), f32[32,24,384]{2,1,0:T(8,128)}, u32[]{:S(2)}, u32[]{:S(2)}) async-start(f32[32,24,384]{2,1,0:T(8,128)} %bitcast.66), calls=%async_computation.2 | async-start | bytes 2359296 | tf_op jit(solution)/shard_map/all_to_all | solution.py:16
  91.0 0.3 all-reduce.3.cloned.1.call-start
  91.3 9.7 %convolution_multiply_fusion = f32[4352,8]{0,1:T(8,128)} fusion(f32[512,4352]{1,0:T(8,128)} %copy-done.1, bf16[512,4352]{1,0:T(8,128)(2,1)} %bitcast.67, f32[4352]{0:T(1024)S(1)} %copy-done.4, pred[512]{0:T(512)(128)(4,1)S(1)} %fusion.26, f32[4,128,8]{1,2,0:T(8,128)S(1)} %copy-done.3), kind=kOutput, calls=%fused_computation.10 | convolution fusion | flops 222857216 | bytes 13542912 | tf_op jit(solution)/shard_map/dot_general | solution.py:77
  100.9 0.0 all-reduce.3.cloned.1.call-update
  101.0 123.9 %all-reduce.3.cloned.1.call-done = f32[4352,8]{0,1:T(8,128)} async-done(((f32[4352,8]{0,1:T(8,128)}), f32[4352,8]{0,1:T(8,128)}) %all-reduce.3.cloned.1.call-update) | async-done | bytes 139280
  224.8 1.4 constant_dynamic-slice_fusion
  226.2 0.0 all-to-all-done.2
  226.2 2.6 %bitcast_multiply_fusion = f32[768,384]{1,0:T(8,128)} fusion(f32[32,24,384]{2,1,0:T(8,128)} %all-to-all-done.2, bf16[768,384]{1,0:T(8,128)(2,1)} %gather_fusion.1), kind=kLoop, calls=%fused_computation.19 | loop fusion | flops 1179648 | bytes 2949120 | tf_op jit(solution)/shard_map/mul | solution.py:73
  228.8 8.4 %scatter_custom_fusion.2 = f32[1024,384]{1,0:T(8,128)} fusion(s32[768]{0:T(1024)S(1)} %fusion.21, f32[768,384]{1,0:T(8,128)} %bitcast_multiply_fusion, f32[]{:T(128)} %constant.50.clone.1), kind=kCustom, calls=%fused_computation.22 | custom fusion | flops 294912 | bytes 1573376 | tf_op jit(solution)/shard_map/scatter-add | solution.py:74
  237.2 2.4 convert_element_type.45
  (8 shorter events, 0.1 us)
Async XLA Ops:
  7.2 56.9 %copy-start = (bf16[384,4352]{1,0:T(8,128)(2,1)S(1)}, bf16[384,4352]{1,0:T(8,128)(2,1)}, u32[]{:S(2)}) copy-start(bf16[384,4352]{1,0:T(8,128)(2,1)} %param.11) | copy-start | bytes 10027012
  33.7 10.2 %copy-start.5 = (s32[4]{0:T(128)S(1)}, s32[4]{0:T(128)}, u32[]{:S(2)}) copy-start(s32[4]{0:T(128)} %param.16) | copy-start | bytes 52
  40.4 20.1 %all-to-all-start.1 = ((bf16[32,24,384]{2,1,0:T(8,128)(2,1)}), bf16[32,24,384]{2,1,0:T(8,128)(2,1)}, u32[]{:S(2)}, u32[]{:S(2)}) async-start(bf16[32,24,384]{2,1,0:T(8,128)(2,1)} %bitcast.72), calls=%async_computation.1 | async-start | bytes 1179648 | tf_op jit(solution)/shard_map/all_to_all | solution.py:12
  64.1 3.6 %copy-start.2 = (f32[8,4352]{1,0:T(8,128)S(1)}, f32[8,4352]{1,0:T(8,128)}, u32[]{:S(2)}) copy-start(f32[8,4352]{1,0:T(8,128)} %param.14) | copy-start | bytes 417796
  64.1 3.7 %copy-start.3 = (f32[4,128,8]{1,2,0:T(8,128)S(1)}, f32[4,128,8]{1,2,0:T(8,128)}, u32[]{:S(2)}) copy-start(f32[4,128,8]{1,2,0:T(8,128)} %param.13) | copy-start | bytes 49156
  64.1 16.3 %slice-start = ((s8[4456448]{0:T(1024)(128)(4,1)}), s8[4194304]{0:T(1024)(128)(4,1)S(1)}, s32[]{:S(2)}) async-start(s8[4456448]{0:T(1024)(128)(4,1)} %bitcast.68), calls=%async_computation.4 | async-start | bytes 8388608
  67.7 12.6 %slice-start.1 = ((s8[4456448]{0:T(1024)(128)(4,1)}), s8[262144]{0:T(1024)(128)(4,1)S(1)}, s32[]{:S(2)}) async-start(s8[4456448]{0:T(1024)(128)(4,1)} %bitcast.68), calls=%async_computation.5 | async-start | bytes 524288
  67.7 12.6 %copy-start.4 = (f32[4352]{0:T(1024)S(1)}, f32[4352]{0:T(1024)}, u32[]{:S(2)}) copy-start(f32[4352]{0:T(1024)} %param.15) | copy-start | bytes 52228
  76.9 3.4 %copy-start.1 = (f32[512,4352]{1,0:T(8,128)}, f32[512,4352]{1,0:T(8,128)S(1)}, u32[]{:S(2)}) copy-start(f32[512,4352]{1,0:T(8,128)S(1)} %get-tuple-element.6) | copy-start | bytes 26738692
  87.6 138.6 %all-to-all-start.2 = ((f32[32,24,384]{2,1,0:T(8,128)}), f32[32,24,384]{2,1,0:T(8,128)}, u32[]{:S(2)}, u32[]{:S(2)}) async-start(f32[32,24,384]{2,1,0:T(8,128)} %bitcast.66), calls=%async_computation.2 | async-start | bytes 2359296 | tf_op jit(solution)/shard_map/all_to_all | solution.py:16
  91.0 133.8 %all-reduce.3.cloned.1.call-start = ((), (), s32[]{:S(2)}) async-start(), calls=%async_computation.3 | async-start | bytes 278528
Sparse Core Ops, SparseCore 0:
  101.1 123.6 all-reduce.2
where the time goes:
time: 248 us; the launch traced here: 246 us
  waiting for transfers between devices  140 us (56%)
  matrix products  25.9 us (10%)
  local copies, waits for them, and re-layouts  24.3 us (10%)
  other arithmetic  20.2 us (8%)
  blocking collectives  14.3 us (6%)
  between operations  14.2 us (6%)
  starting transfers between devices  7.15 us (3%)
    unnamed x2, waiting for transfers between devices  124 us
    all_to_all x1, waiting for transfers between devices, route_profiles(): lax.all_to_all(payload, ('lat', 'lon'), split_axis=0, concat_axis=0, tile...  16.5 us
    all_to_all x1, blocking collectives, route_ids(): lax.all_to_all(requests, ('lat', 'lon'), split_axis=0, concat_axis=0, til...  14.3 us
    dot_general x1, matrix products, shards(): lax.dot_general(misfit, flat_pred, (((0,), (0,)), ((), ())), precision=la...  9.67 us
    dot_general x1, matrix products, shards(): jnp.dot(flat_pred, beta_incr, precision=lax.Precision.HIGHEST)  9.19 us
    scatter-add x1, other arithmetic, shards(): jnp.zeros((column_count, profile_len), jnp.float32).at[wanted].add(returned)  8.4 us
  transfers between devices with their start and end apart: 3, of which 2 were waited for; matrix products, arithmetic and copies ran while one was open for 5% of the time, Pallas kernels for 0%

commit v1 on v0

--- a/solution.py
+++ b/solution.py
@@ -68,18 +68,22 @@
         (((1,), (1,)), ((), ())),
         preferred_element_type=jnp.float32,
     )
-    outgoing = jnp.zeros((devices * capacity, profile_len), jnp.float32).at[position].set(pulled)
+    outgoing = jnp.zeros((devices * capacity, profile_len), jnp.bfloat16).at[position].set(
+        pulled.astype(jnp.bfloat16)
+    )
     returned = route_adjoint(outgoing.reshape(devices, capacity, profile_len))
-    returned = returned.reshape(devices * capacity, profile_len) * owner_jacobian
+    returned = returned.reshape(devices * capacity, profile_len).astype(jnp.float32) * owner_jacobian
     gradient = jnp.zeros((column_count, profile_len), jnp.float32).at[wanted].add(returned)
     column_grad = gradient.astype(jnp.bfloat16)
     local_bias = (
         lax.dot_general(
-            misfit, flat_pred, (((0,), (0,)), ((), ())), precision=lax.Precision.HIGHEST
+            flat_pred, misfit, (((0,), (0,)), ((), ())), precision=lax.Precision.HIGHEST
         )
         * scaling
     )
-    bias_grad = lax.psum_scatter(local_bias, ("lat", "lon"), scatter_dimension=0, tiled=True)
+    pieces = local_bias.reshape(npredictors, devices, channels // devices).transpose(1, 0, 2)
+    shares = lax.all_to_all(pieces, ("lat", "lon"), split_axis=0, concat_axis=0, tiled=True)
+    bias_grad = jnp.sum(shares, axis=0).T
     return (radiance, column_grad, bias_grad)
 
 

time: 248 us -> 132 us (0.53)
  waiting for transfers between devices: 140 us -> 31.7 us
  between operations: 14.2 us -> 0.8 us
  starting transfers between devices: 7.15 us -> 12.7 us
    unnamed x2 -> x0, waiting for transfers between devices: 124 us -> none
    all_to_all x1, waiting for transfers between devices: 0.01 us -> 15 us  [route_adjoint(): lax.all_to_all(payload, ('lat', 'lon'), split_axis=0, concat_axis=0, tile...]
    dot_general x1, matrix products: 3.39 us -> 8.05 us  [shards(): lax.dot_general(misfit.astype(jnp.bfloat16), coefficients, (((1,), (1,)),...]
    dot_general x1, matrix products: 9.67 us -> 5.93 us  [shards(): lax.dot_general(flat_pred, misfit, (((0,), (0,)), ((), ())), precision=la...]
    all_to_all x0 -> x1, starting transfers between devices: none -> 3.31 us  [shards(): lax.all_to_all(pieces, ('lat', 'lon'), split_axis=0, concat_axis=0, tiled...]
    reshape x0 -> x2, local copies, waits for them, and re-layouts: none -> 2.83 us  [shards(): local_bias.reshape(npredictors, devices, channels // devices)]
    all_to_all x1, starting transfers between devices: 3.39 us -> 6.1 us  [route_adjoint(): lax.all_to_all(payload, ('lat', 'lon'), split_axis=0, concat_axis=0, tile...]
    mul x1 -> x0, other arithmetic: 2.63 us -> none  [shards(): returned.reshape(devices * capacity, profile_len) * owner_jacobian]
  transfers between devices with their start and end apart: 3 -> 3, of which waited for: 2 -> 2; matrix products, arithmetic and copies ran while one was open for 5% -> 10% of each run, Pallas kernels for 0% -> 0%
where the time goes in v1:
time: 132 us
  waiting for transfers between devices  31.7 us (24%)
  matrix products  27.1 us (21%)
  local copies, waits for them, and re-layouts  25.6 us (19%)
  other arithmetic  19.5 us (15%)
  blocking collectives  14.3 us (11%)
  starting transfers between devices  12.7 us (10%)
    all_to_all x1, waiting for transfers between devices, route_profiles(): lax.all_to_all(payload, ('lat', 'lon'), split_axis=0, concat_axis=0, tile...  16.7 us
    all_to_all x1, waiting for transfers between devices, route_adjoint(): lax.all_to_all(payload, ('lat', 'lon'), split_axis=0, concat_axis=0, tile...  15 us
    all_to_all x1, blocking collectives, route_ids(): lax.all_to_all(requests, ('lat', 'lon'), split_axis=0, concat_axis=0, til...  14.3 us
    dot_general x1, matrix products, shards(): jnp.dot(flat_pred, beta_incr, precision=lax.Precision.HIGHEST)  9.53 us
    scatter-add x1, other arithmetic, shards(): jnp.zeros((column_count, profile_len), jnp.float32).at[wanted].add(returned)  8.7 us
    dot_general x1, matrix products, shards(): lax.dot_general(misfit.astype(jnp.bfloat16), coefficients, (((1,), (1,)),...  8.05 us
    all_to_all x1, starting transfers between devices, route_adjoint(): lax.all_to_all(payload, ('lat', 'lon'), split_axis=0, concat_axis=0, tile...  6.1 us
    dot_general x1, matrix products, shards(): lax.dot_general(flat_pred, misfit, (((0,), (0,)), ((), ())), precision=la...  5.93 us
  transfers between devices with their start and end apart: 3, of which 2 were waited for; matrix products, arithmetic and copies ran while one was open for 10% of the time, Pallas kernels for 0%

profile of v1, /device:TPU:0, one launch (start us, length us, event | category | flops | bytes accessed | tf_op | source)
XLA Modules:
  0.0 131.7 jit_solution(14985623513714067053)
XLA Ops:
  0.6 0.0 copy-start
  0.6 0.8 add_select_fusion.2
  1.5 0.9 add_select_fusion.1
  2.4 1.2 reduce-window.6
  3.5 0.2 slice_reduce_fusion
  3.8 0.1 fusion.23
  3.9 0.7 compare_select_fusion.1
  4.6 2.4 %scatter_custom_fusion = s32[768]{0:T(1024)S(1)} fusion(s32[512]{0:T(512)S(1)} %bitcast.81, s32[512]{0:T(512)S(1)} %get-tuple-element.3, s32[]{:T(128)} %constant.40.clone.1), kind=kCustom, calls=%fused_computation.64 | custom fusion | bytes 3076 | tf_op jit(solution)/shard_map/scatter | solution.py:48
  7.1 0.1 all_to_all.15
  7.2 14.3 %all_to_all.24 = s32[32,1,24]{2,1,0:T(1,128)S(1)} all-to-all(s32[32,1,24]{2,1,0:T(1,128)S(1)} %bitcast.78), channel_id=1, replica_groups=mesh['lat'=4,'lon'=8] {'lat','lon'}, dimensions={0} | all-to-all | bytes 6144 | tf_op jit(solution)/shard_map/all_to_all | solution.py:8
  21.5 0.5 broadcast.226
  22.0 0.7 reduce.7
  22.7 0.1 reshape.218
  22.8 4.4 %gather_fusion.1 = bf16[768,384]{1,0:T(8,128)(2,1)} fusion(bf16[1024,384]{1,0:T(8,128)(2,1)} %param.9, s32[1024]{0:T(1024)S(1)} %pad_clamp_fusion.1), kind=kCustom, calls=%fused_computation.1 | custom fusion | bytes 1182720 | tf_op jit(solution)/shard_map/gather | solution.py:50
  27.2 0.0 copy-start.5
  27.2 4.4 %gather_fusion = bf16[768,384]{1,0:T(8,128)(2,1)} fusion(bf16[1024,384]{1,0:T(8,128)(2,1)} %param.10, s32[1024]{0:T(1024)S(1)} %pad_clamp_fusion.1), kind=kCustom, calls=%fused_computation | custom fusion | bytes 1182720 | tf_op jit(solution)/shard_map/gather | solution.py:51
  31.5 2.3 %multiply_convert_fusion = bf16[768,384]{1,0:T(8,128)(2,1)} fusion(bf16[768,384]{1,0:T(8,128)(2,1)} %gather_fusion, bf16[768,384]{1,0:T(8,128)(2,1)} %gather_fusion.1), kind=kLoop, calls=%fused_computation.23 | loop fusion | flops 1769472 | bytes 1769472 | tf_op jit(solution)/shard_map/convert_element_type | solution.py:53
  33.8 3.3 %all-to-all-start.1 = ((bf16[32,24,384]{2,1,0:T(8,128)(2,1)}), bf16[32,24,384]{2,1,0:T(8,128)(2,1)}, u32[]{:S(2)}, u32[]{:S(2)}) async-start(bf16[32,24,384]{2,1,0:T(8,128)(2,1)} %bitcast.75), calls=%async_computation.1 | async-start | bytes 1179648 | tf_op jit(solution)/shard_map/all_to_all | solution.py:12
  37.2 0.0 copy-done.5
  37.2 0.1 fusion.32
  37.3 16.7 %all-to-all-done.1 = bf16[32,24,384]{2,1,0:T(8,128)(2,1)} async-done(((bf16[32,24,384]{2,1,0:T(8,128)(2,1)}), bf16[32,24,384]{2,1,0:T(8,128)(2,1)}, u32[]{:S(2)}, u32[]{:S(2)}) %all-to-all-start.1) | async-done | bytes 589856 | tf_op jit(solution)/shard_map/all_to_all | solution.py:12
  54.0 3.6 %gather_fusion.2 = bf16[512,384]{1,0:T(8,128)(2,1)} fusion(bf16[768,384]{1,0:T(8,128)(2,1)} %bitcast.8, s32[1024]{0:T(1024)S(1)} %pad_clamp_fusion), kind=kCustom, calls=%fused_computation.2 | custom fusion | bytes 788480 | tf_op jit(solution)/shard_map/gather | solution.py:55
  57.5 0.0 copy-done
  57.6 0.0 copy-start.2
  57.6 0.0 copy-start.3
  57.6 0.0 slice-start
  57.6 3.6 %fusion.38 = f32[512,4352]{1,0:T(8,128)S(1)} fusion(bf16[512,384]{1,0:T(8,128)(2,1)} %gather_fusion.2, bf16[384,4352]{1,0:T(8,128)(2,1)S(1)} %copy-done), kind=kOutput, calls=%fused_computation.75 | convolution fusion | flops 1711276032 | bytes 12648448 | tf_op jit(solution)/shard_map/dot_general | solution.py:59
  61.2 0.0 copy-done.2
  61.2 0.0 copy-done.3
  61.2 0.0 slice-start.1
  61.2 0.0 copy-start.4
  61.2 9.5 %fusion.37 = (bf16[512,4352]{1,0:T(8,128)(2,1)}, f32[512,4352]{1,0:T(8,128)S(1)}) fusion(f32[512,4352]{1,0:T(8,128)S(1)} %fusion.38, f32[8,4352]{1,0:T(8,128)S(1)} %copy-done.2, f32[4,128,8]{1,2,0:T(8,128)S(1)} %copy-done.3, pred[512]{0:T(512)(128)(4,1)S(1)} %fusion.32), kind=kOutput, calls=%fused_computation.74 | convolution fusion | flops 220594176 | bytes 22438400 | tf_op jit(solution)/shard_map/dot_general | solution.py:60
  70.8 0.0 copy-start.1
  70.8 3.4 %copy-done.1 = f32[512,4352]{1,0:T(8,128)} copy-done((f32[512,4352]{1,0:T(8,128)}, f32[512,4352]{1,0:T(8,128)S(1)}, u32[]{:S(2)}) %copy-start.1) | copy-done | bytes 8912920
  74.2 0.0 slice-done
  74.2 0.0 slice-done.1
  74.2 0.0 copy-done.4
  74.2 5.9 %fusion.2 = f32[8,4352]{1,0:T(8,128)S(1)} fusion(f32[512,4352]{1,0:T(8,128)S(1)} %get-tuple-element.6, bf16[512,4352]{1,0:T(8,128)(2,1)S(1)} %bitcast.73, f32[4352]{0:T(1024)S(1)} %copy-done.4, pred[512]{0:T(512)(128)(4,1)S(1)} %fusion.32, f32[4,128,8]{1,2,0:T(8,128)S(1)} %copy-done.3), kind=kOutput, calls=%fused_computation.11 | convolution fusion | flops 222857216 | bytes 13542912 | tf_op jit(solution)/shard_map/dot_general | solution.py:79
  80.1 1.0 reshape.223
  81.2 1.8 %copy.19 = f32[8,32,136]{2,0,1:T(8,128)} copy(f32[8,32,136]{2,1,0:T(8,128)} %reshape.223) | data formatting | bytes 278528 | tf_op jit(solution)/shard_map/reshape | solution.py:84
  83.0 3.3 %all-to-all-start.3 = ((f32[32,8,136]{2,1,0:T(8,128)}), f32[32,8,136]{2,1,0:T(8,128)}, u32[]{:S(2)}, u32[]{:S(2)}) async-start(f32[32,8,136]{2,1,0:T(8,128)} %bitcast.77), calls=%async_computation.3 | async-start | bytes 524288 | tf_op jit(solution)/shard_map/all_to_all | solution.py:85
  86.3 8.0 %fusion.13 = bf16[512,384]{1,0:T(8,128)(2,1)} fusion(bf16[384,4352]{1,0:T(8,128)(2,1)S(1)} %copy-done, f32[512,4352]{1,0:T(8,128)} %copy-done.1, bf16[512,4352]{1,0:T(8,128)(2,1)} %bitcast.70, f32[4352]{0:T(1024)S(1)} %copy-done.4, pred[512]{0:T(512)(128)(4,1)S(1)} %fusion.32), kind=kOutput, calls=%fused_computation.20 | convolution fusion | flops 1722613760 | bytes 17122816 | tf_op jit(solution)/shard_map/dot_general | solution.py:65
  94.3 3.6 %scatter_custom_fusion.1 = bf16[768,384]{1,0:T(8,128)(2,1)} fusion(s32[512]{0:T(512)S(1)} %bitcast.83, bf16[512,384]{1,0:T(8,128)(2,1)} %fusion.13, bf16[]{:T(256)} %constant.51.clone.1), kind=kCustom, calls=%fused_computation.28 | custom fusion | bytes 590336 | tf_op jit(solution)/shard_map/scatter | solution.py:71
  98.0 0.0 all-to-all-done.3
  98.0 6.1 %all-to-all-start.2 = ((bf16[32,24,384]{2,1,0:T(8,128)(2,1)}), bf16[32,24,384]{2,1,0:T(8,128)(2,1)}, u32[]{:S(2)}, u32[]{:S(2)}) async-start(bf16[32,24,384]{2,1,0:T(8,128)(2,1)} %bitcast.76), calls=%async_computation.2 | async-start | bytes 1179648 | tf_op jit(solution)/shard_map/all_to_all | solution.py:16
  104.1 1.6 %reduce_sum.19 = f32[8,136]{1,0:T(8,128)} reduce(f32[32,8,136]{2,1,0:T(8,128)} %all-to-all-done.3, f32[]{:T(128)} %constant.50.clone.1), dimensions={0}, to_apply=%region_6.7 | reduce | flops 33728 | bytes 143620 | tf_op jit(solution)/shard_map/reduce_sum | solution.py:86
  105.7 15.0 %all-to-all-done.2 = bf16[32,24,384]{2,1,0:T(8,128)(2,1)} async-done(((bf16[32,24,384]{2,1,0:T(8,128)(2,1)}), bf16[32,24,384]{2,1,0:T(8,128)(2,1)}, u32[]{:S(2)}, u32[]{:S(2)}) %all-to-all-start.2) | async-done | bytes 589856 | tf_op jit(solution)/shard_map/all_to_all | solution.py:16
  120.6 8.7 %scatter_custom_fusion.2 = f32[1024,384]{1,0:T(8,128)} fusion(s32[768]{0:T(1024)S(1)} %fusion.27, bf16[768,384]{1,0:T(8,128)(2,1)} %bitcast.18, bf16[768,384]{1,0:T(8,128)(2,1)} %gather_fusion.1, f32[]{:T(128)} %constant.50.clone.1, f32[]{:T(128)} %constant.49.clone.1, f32[]{:T(128)} %constant.48.clone.1), kind=kCustom, calls=%fused_computation.22 | custom fusion | flops 1769472 | bytes 2752524 | tf_op jit(solution)/shard_map/scatter-add | solution.py:76
  129.3 2.4 %convert_element_type.57 = bf16[1024,384]{1,0:T(8,128)(2,1)} convert(f32[1024,384]{1,0:T(8,128)} %scatter_custom_fusion.2) | non-fusion elementwise | flops 393216 | bytes 2359296 | tf_op jit(solution)/shard_map/convert_element_type | solution.py:77
  (8 shorter events, 0.1 us)
Async XLA Ops:
  0.6 56.9 %copy-start = (bf16[384,4352]{1,0:T(8,128)(2,1)S(1)}, bf16[384,4352]{1,0:T(8,128)(2,1)}, u32[]{:S(2)}) copy-start(bf16[384,4352]{1,0:T(8,128)(2,1)} %param.11) | copy-start | bytes 10027012
  27.2 10.0 %copy-start.5 = (s32[4]{0:T(128)S(1)}, s32[4]{0:T(128)}, u32[]{:S(2)}) copy-start(s32[4]{0:T(128)} %param.16) | copy-start | bytes 52
  33.8 20.1 %all-to-all-start.1 = ((bf16[32,24,384]{2,1,0:T(8,128)(2,1)}), bf16[32,24,384]{2,1,0:T(8,128)(2,1)}, u32[]{:S(2)}, u32[]{:S(2)}) async-start(bf16[32,24,384]{2,1,0:T(8,128)(2,1)} %bitcast.75), calls=%async_computation.1 | async-start | bytes 1179648 | tf_op jit(solution)/shard_map/all_to_all | solution.py:12
  57.6 3.6 %copy-start.2 = (f32[8,4352]{1,0:T(8,128)S(1)}, f32[8,4352]{1,0:T(8,128)}, u32[]{:S(2)}) copy-start(f32[8,4352]{1,0:T(8,128)} %param.14) | copy-start | bytes 417796
  57.6 3.7 %copy-start.3 = (f32[4,128,8]{1,2,0:T(8,128)S(1)}, f32[4,128,8]{1,2,0:T(8,128)}, u32[]{:S(2)}) copy-start(f32[4,128,8]{1,2,0:T(8,128)} %param.13) | copy-start | bytes 49156
  57.6 16.6 %slice-start = ((s8[4456448]{0:T(1024)(128)(4,1)}), s8[4194304]{0:T(1024)(128)(4,1)S(1)}, s32[]{:S(2)}) async-start(s8[4456448]{0:T(1024)(128)(4,1)} %bitcast.71), calls=%async_computation.4 | async-start | bytes 8388608
  61.2 13.0 %slice-start.1 = ((s8[4456448]{0:T(1024)(128)(4,1)}), s8[262144]{0:T(1024)(128)(4,1)S(1)}, s32[]{:S(2)}) async-start(s8[4456448]{0:T(1024)(128)(4,1)} %bitcast.71), calls=%async_computation.5 | async-start | bytes 524288
  61.2 13.0 %copy-start.4 = (f32[4352]{0:T(1024)S(1)}, f32[4352]{0:T(1024)}, u32[]{:S(2)}) copy-start(f32[4352]{0:T(1024)} %param.15) | copy-start | bytes 52228
  70.8 3.4 %copy-start.1 = (f32[512,4352]{1,0:T(8,128)}, f32[512,4352]{1,0:T(8,128)S(1)}, u32[]{:S(2)}) copy-start(f32[512,4352]{1,0:T(8,128)S(1)} %get-tuple-element.6) | copy-start | bytes 26738692
  83.0 15.0 %all-to-all-start.3 = ((f32[32,8,136]{2,1,0:T(8,128)}), f32[32,8,136]{2,1,0:T(8,128)}, u32[]{:S(2)}, u32[]{:S(2)}) async-start(f32[32,8,136]{2,1,0:T(8,128)} %bitcast.77), calls=%async_computation.3 | async-start | bytes 524288 | tf_op jit(solution)/shard_map/all_to_all | solution.py:85
  98.0 22.7 %all-to-all-start.2 = ((bf16[32,24,384]{2,1,0:T(8,128)(2,1)}), bf16[32,24,384]{2,1,0:T(8,128)(2,1)}, u32[]{:S(2)}, u32[]{:S(2)}) async-start(bf16[32,24,384]{2,1,0:T(8,128)(2,1)} %bitcast.76), calls=%async_computation.2 | async-start | bytes 1179648 | tf_op jit(solution)/shard_map/all_to_all | solution.py:16

commit v2 on v0

v2 whole, which is shorter than its diff:
```python
import functools

import jax
import jax.numpy as jnp
from jax import lax
from jax.experimental import pallas as pl
from jax.experimental.pallas import tpu as pltpu
from jax.sharding import PartitionSpec as P

MESH = pl.DeviceIdType.MESH
VMEM = pl.BlockSpec(memory_space=pltpu.VMEM)
SPAN = 128
GRANT = 60 * 1024 * 1024


def peers_of(lat_count, lon_count):
    devices = lat_count * lon_count
    me = lax.axis_index("lat") * lon_count + lax.axis_index("lon")

    def peer(offset):
        other = lax.rem(me + offset, devices)
        return other, (lax.div(other, lon_count), lax.rem(other, lon_count))

    return me, peer


def greet(devices, peer):
    barrier = pltpu.get_barrier_semaphore()

    def one(offset, carry):
        pl.semaphore_signal(barrier, inc=1, device_id=peer(offset)[1], device_id_type=MESH)
        return carry

    lax.fori_loop(1, devices, one, 0)
    return barrier


def send_all(devices, me, peer, source, target, send_sem, recv_sem):
    def one(offset, carry):
        other, where = peer(offset)
        pltpu.make_async_remote_copy(
            src_ref=source.at[other],
            dst_ref=target.at[me],
            send_sem=send_sem.at[offset],
            recv_sem=recv_sem.at[me],
            device_id=where,
            device_id_type=MESH,
        ).start()
        return carry

    lax.fori_loop(1, devices, one, 0)


def wait_all(devices, peer, source, target, send_sem, recv_sem):
    def one(offset, carry):
        other, where = peer(offset)
        copy = pltpu.make_async_remote_copy(
            src_ref=source.at[other],
            dst_ref=target.at[other],
            send_sem=send_sem.at[offset],
            recv_sem=recv_sem.at[other],
            device_id=where,
            device_id_type=MESH,
        )
        copy.wait_recv()
        copy.wait_send()
        return carry

    lax.fori_loop(1, devices, one, 0)


def iota(shape, dim):
    return lax.broadcasted_iota(jnp.int32, shape, dim)


def ones_where(mask):
    return jnp.where(mask, jnp.float32(1.0), jnp.float32(0.0)).astype(jnp.bfloat16)


def dot(a, b):
    return jnp.dot(a, b, preferred_element_type=jnp.float32)


def dot_nt(a, b):
    return lax.dot_general(a, b, (((1,), (1,)), ((), ())), preferred_element_type=jnp.float32)


def fetch_kernel(
    lat_count,
    lon_count,
    capacity,
    cols_ref,
    base_ref,
    step_ref,
    pred_ref,
    position_ref,
    wanted_ref,
    ask,
    asked,
    formed,
    outbound,
    inbound,
    picker,
    ask_send,
    ask_recv,
    row_send,
    row_recv,
):
    devices = lat_count * lon_count
    column_count, profile_len = base_ref.shape
    slots = cols_ref.shape[1]
    rows = devices * capacity
    shift = column_count.bit_length() - 1
    assert column_count == 1 << shift
    me, peer = peers_of(lat_count, lon_count)
    barrier = greet(devices, peer)

    cols = cols_ref[...]
    owners = lax.shift_right_logical(cols, shift)
    local = cols & (column_count - 1)
    owned = jnp.where(iota((devices, slots), 0) == owners, jnp.float32(1.0), jnp.float32(0.0))
    before = ones_where(iota((slots, slots), 0) < iota((slots, slots), 1))
    ranks = dot(owned.astype(jnp.bfloat16), before)
    rank = jnp.sum(owned * ranks, axis=0, keepdims=True).astype(jnp.int32)
    position = owners * capacity + rank
    position_ref[...] = position
    spot = ones_where(iota((SPAN, slots), 0) == rank)
    high = lax.shift_right_logical(local, 8).astype(jnp.float32)
    low = (local & 255).astype(jnp.float32)
    asks = dot_nt((owned * high).astype(jnp.bfloat16), spot) * 256.0
    asks = asks + dot_nt((owned * low).astype(jnp.bfloat16), spot)
    ask[:, 0, :] = asks

    pl.semaphore_wait(barrier, devices - 1)
    send_all(devices, me, peer, ask, asked, ask_send, ask_recv)
    asked[me] = ask[me]
    jacobian = 1.0 + 0.5 * jnp.tanh(base_ref[...].astype(jnp.float32))
    formed[...] = (step_ref[...].astype(jnp.float32) * jacobian).astype(jnp.bfloat16)
    wait_all(devices, peer, ask, asked, ask_send, ask_recv)

    table = asked[:, 0, :].astype(jnp.int32)
    first = iota((rows, devices), 1) * capacity
    row = iota((rows, devices), 0)
    spread = ones_where((row >= first) & (row < first + capacity))
    table_high = lax.shift_right_logical(table, 8).astype(jnp.float32).astype(jnp.bfloat16)
    table_low = (table & 255).astype(jnp.float32).astype(jnp.bfloat16)
    listed = dot(spread, table_high) * 256.0 + dot(spread, table_low)
    row_f = iota((rows, SPAN), 0).astype(jnp.float32)
    within = row_f - capacity * jnp.floor((row_f + 0.5) * (1.0 / capacity))
    lane_f = iota((rows, SPAN), 1).astype(jnp.float32)
    wanted = jnp.sum(jnp.where(lane_f == within, listed, 0.0), axis=1, keepdims=True)
    wanted = wanted.astype(jnp.int32)
    chosen = ones_where(wanted == iota((rows, column_count), 1))
    payload = dot(chosen, formed[...]).reshape(devices, capacity, profile_len)
    outbound[...] = payload.astype(jnp.bfloat16)
    send_all(devices, me, peer, outbound, inbound, row_send, row_recv)
    inbound[me] = outbound[me]

    diagonal = iota((rows, rows), 0) == iota((rows, rows), 1)
    wanted_f = wanted.astype(jnp.float32)
    wanted_ref[...] = jnp.sum(
        jnp.where(diagonal, wanted_f, 0.0), axis=0, keepdims=True
    ).astype(jnp.int32)
    diagonal = iota((slots, slots), 0) == iota((slots, slots), 1)
    upright = jnp.sum(
        jnp.where(diagonal, position.astype(jnp.float32), 0.0), axis=1, keepdims=True
    ).astype(jnp.int32)
    picker[...] = ones_where(upright == iota((slots, rows), 1))
    wait_all(devices, peer, outbound, inbound, row_send, row_recv)
    arrived = inbound[...].astype(jnp.float32).reshape(rows, profile_len).astype(jnp.bfloat16)
    pred_ref[...] = dot(picker[...], arrived).astype(jnp.bfloat16)


def fetch(lat_count, lon_count, capacity, cols, background, increment):
    devices = lat_count * lon_count
    column_count, profile_len = background.shape
    slots = cols.shape[1]
    rows = devices * capacity
    return pl.pallas_call(
        functools.partial(fetch_kernel, lat_count, lon_count, capacity),
        out_shape=(
            jax.ShapeDtypeStruct((slots, profile_len), jnp.bfloat16),
            jax.ShapeDtypeStruct((1, slots), jnp.int32),
            jax.ShapeDtypeStruct((1, rows), jnp.int32),
        ),
        in_specs=[VMEM] * 3,
        out_specs=(VMEM,) * 3,
        scratch_shapes=[
            pltpu.VMEM((devices, 1, SPAN), jnp.float32),
            pltpu.VMEM((devices, 1, SPAN), jnp.float32),
            pltpu.VMEM((column_count, profile_len), jnp.bfloat16),
            pltpu.VMEM((devices, capacity, profile_len), jnp.bfloat16),
            pltpu.VMEM((devices, capacity, profile_len), jnp.bfloat16),
            pltpu.VMEM((slots, rows), jnp.bfloat16),
        ]
        + [pltpu.SemaphoreType.DMA((devices,))] * 4,
        compiler_params=pltpu.CompilerParams(
            collective_id=0, has_side_effects=True, vmem_limit_bytes=GRANT
        ),
        name="fetch_profiles",
    )(cols, background, increment)


def compute_kernel(
    block_len,
    scaling,
    count_ref,
    pred_ref,
    aug_ref,
    flip_ref,
    coef_ref,
    dep_ref,
    beta_ref,
    weight_ref,
    rad_ref,
    pulled_ref,
    bias_ref,
    left,
    total,
    main,
    rest,
):
    step = pl.program_id(0)
    profile_len = pred_ref.shape[1]
    npredictors, tile = beta_ref.shape

    @pl.when(step == 0)
    def _():
        left[:, :profile_len] = pred_ref[...]
        left[:, profile_len:] = aug_ref[...]
        total[...] = jnp.zeros_like(total)

    coef = coef_ref[...]
    beta = beta_ref[...]
    beta_main = beta.astype(jnp.bfloat16).astype(jnp.float32)
    beta_rest = beta - beta_main
    filler = jnp.zeros((SPAN - 3 * npredictors, tile), jnp.float32)
    extra = jnp.concatenate([beta_main, beta_rest, beta_main, filler], axis=0)
    right = jnp.concatenate([coef, extra.astype(jnp.bfloat16)], axis=0)
    weight = weight_ref[...]
    for block in range(pred_ref.shape[0] // block_len):
        part = pl.ds(block * block_len, block_len)
        present = iota((block_len, tile), 0) < count_ref[block]
        radiance = jnp.where(present, dot(left[part, :], right), 0.0)
        rad_ref[part, :] = radiance.astype(jnp.bfloat16)
        misfit = weight * (radiance - dep_ref[part, :].astype(jnp.float32))
        misfit = jnp.where(present, misfit, 0.0)
        misfit_b = misfit.astype(jnp.bfloat16)
        main[part, :] = misfit_b
        rest[part, :] = (misfit - misfit_b.astype(jnp.float32)).astype(jnp.bfloat16)
    total[...] += dot_nt(main[...], coef)
    whole = dot(flip_ref[...], main[...])
    small = dot(flip_ref[...], rest[...])
    bias_ref[...] = scaling * (
        whole[:npredictors] + whole[npredictors:] + small[:npredictors]
    )

    @pl.when(step == pl.num_programs(0) - 1)
    def _():
        pulled_ref[...] = total[...].astype(jnp.bfloat16)


def compute(block_len, scaling, obs_count, pred, flat_pred, coef, dep, beta, weight):
    slots, profile_len = pred.shape
    channels = coef.shape[1]
    npredictors = flat_pred.shape[1]
    tile = max(t for t in range(128, 513, 128) if channels % t == 0)
    main = lax.reduce_precision(flat_pred, 8, 7)
    rest = (flat_pred - main).astype(jnp.bfloat16)
    main = main.astype(jnp.bfloat16)
    filler = jnp.zeros((slots, SPAN - 3 * npredictors), jnp.bfloat16)
    aug = jnp.concatenate([main, main, rest, filler], axis=1)
    flip = jnp.concatenate([main, rest], axis=1).T

    def fixed(shape):
        return pl.BlockSpec(shape, lambda i: (0, 0))

    def moving(height):
        return pl.BlockSpec((height, tile), lambda i: (0, i))

    return pl.pallas_call(
        functools.partial(compute_kernel, block_len, scaling),
        grid=(channels // tile,),
        out_shape=(
            jax.ShapeDtypeStruct((slots, channels), jnp.bfloat16),
            jax.ShapeDtypeStruct((slots, profile_len), jnp.bfloat16),
            jax.ShapeDtypeStruct((npredictors, channels), jnp.float32),
        ),
        in_specs=[
            pl.BlockSpec(memory_space=pltpu.SMEM),
            fixed((slots, profile_len)),
            fixed((slots, SPAN)),
            fixed((2 * npredictors, slots)),
            moving(profile_len),
            moving(slots),
            moving(npredictors),
            moving(1),
        ],
        out_specs=(moving(slots), fixed((slots, profile_len)), moving(npredictors)),
        scratch_shapes=[
            pltpu.VMEM((slots, profile_len + SPAN), jnp.bfloat16),
            pltpu.VMEM((slots, profile_len), jnp.float32),
            pltpu.VMEM((slots, tile), jnp.bfloat16),
            pltpu.VMEM((slots, tile), jnp.bfloat16),
        ],
        compiler_params=pltpu.CompilerParams(vmem_limit_bytes=GRANT),
        name="operator",
    )(obs_count, pred, aug, flip, coef, dep, beta, weight)


def return_kernel(
    lat_count,
    lon_count,
    capacity,
    pulled_ref,
    position_ref,
    wanted_ref,
    bias_ref,
    base_ref,
    grad_ref,
    sum_ref,
    outbound,
    inbound,
    shares,
    collector,
    jacobian,
    row_send,
    row_recv,
    bias_send,
    bias_recv,
):
    devices = lat_count * lon_count
    column_count, profile_len = base_ref.shape
    slots = pulled_ref.shape[0]
    rows = devices * capacity
    me, peer = peers_of(lat_count, lon_count)
    barrier = greet(devices, peer)
    placed = ones_where(iota((rows, slots), 0) == position_ref[...])
    payload = dot(placed, pulled_ref[...]).reshape(devices, capacity, profile_len)
    outbound[...] = payload.astype(jnp.bfloat16)
    pl.semaphore_wait(barrier, devices - 1)
    send_all(devices, me, peer, outbound, inbound, row_send, row_recv)
    send_all(devices, me, peer, bias_ref, shares, bias_send, bias_recv)
    inbound[me] = outbound[me]
    shares[me] = bias_ref[me]
    collector[...] = ones_where(iota((column_count, rows), 0) == wanted_ref[...])
    jacobian[...] = 1.0 + 0.5 * jnp.tanh(base_ref[...].astype(jnp.float32))
    wait_all(devices, peer, outbound, inbound, row_send, row_recv)
    arrived = inbound[...].astype(jnp.float32).reshape(rows, profile_len).astype(jnp.bfloat16)
    grad_ref[...] = (dot(collector[...], arrived) * jacobian[...]).astype(jnp.bfloat16)
    wait_all(devices, peer, bias_ref, shares, bias_send, bias_recv)
    sum_ref[...] = jnp.sum(shares[...], axis=0)


def give_back(lat_count, lon_count, capacity, pulled, position, wanted, bias, background):
    devices = lat_count * lon_count
    column_count, profile_len = background.shape
    rows = devices * capacity
    return pl.pallas_call(
        functools.partial(return_kernel, lat_count, lon_count, capacity),
        out_shape=(
            jax.ShapeDtypeStruct(background.shape, jnp.bfloat16),
            jax.ShapeDtypeStruct(bias.shape[1:], jnp.float32),
        ),
        in_specs=[VMEM] * 5,
        out_specs=(VMEM,) * 2,
        scratch_shapes=[
            pltpu.VMEM((devices, capacity, profile_len), jnp.bfloat16),
            pltpu.VMEM((devices, capacity, profile_len), jnp.bfloat16),
            pltpu.VMEM(bias.shape, jnp.float32),
            pltpu.VMEM((column_count, rows), jnp.bfloat16),
            pltpu.VMEM((column_count, profile_len), jnp.float32),
        ]
        + [pltpu.SemaphoreType.DMA((devices,))] * 4,
        compiler_params=pltpu.CompilerParams(
            collective_id=1, has_side_effects=True, vmem_limit_bytes=GRANT
        ),
        name="return_adjoint",
    )(pulled, position, wanted, bias, background)


def shards(
    background,
    increment,
    coefficients,
    departures,
    bias_pred,
    beta_incr,
    obs_weight,
    obs_count,
    col_index,
):
    lat_count = lax.axis_size("lat")
    lon_count = lax.axis_size("lon")
    devices = lat_count * lon_count
    block_count, block_len = col_index.shape
    channels = coefficients.shape[1]
    npredictors = bias_pred.shape[2]
    slot_count = block_count * block_len
    capacity = 8 * pl.cdiv(3 * slot_count // (2 * devices), 8)
    scaling = (slot_count * devices) ** -0.5
    pred, position, wanted = fetch(
        lat_count, lon_count, capacity, col_index.reshape(1, slot_count), background, increment
    )
    radiance, pulled, bias = compute(
        block_len,
        scaling,
        obs_count,
        pred,
        bias_pred.reshape(slot_count, npredictors),
        coefficients,
        departures.reshape(slot_count, channels),
        beta_incr,
        obs_weight.reshape(1, channels),
    )
    bias = bias.reshape(npredictors, devices, channels // devices).transpose(1, 0, 2)
    column_grad, bias_grad = give_back(
        lat_count, lon_count, capacity, pulled, position, wanted, bias, background
    )
    return (radiance.reshape(departures.shape), column_grad, bias_grad.T)


def solution(mesh):
    return jax.shard_map(
        shards,
        mesh=mesh,
        in_specs=(
            P(("lat", "lon"), None),
            P(("lat", "lon"), None),
            P(),
            P(("lat", "lon"), None, None),
            P(("lat", "lon"), None, None),
            P(),
            P(),
            P(("lat", "lon")),
            P(("lat", "lon"), None),
        ),
        out_specs=(P(("lat", "lon"), None, None), P(("lat", "lon"), None), P(("lat", "lon"), None)),
        check_vma=False,
    )
```

time: 248 us -> 82.5 us (0.33)
  waiting for transfers between devices: 140 us -> 0 us
  Pallas kernels: 0 us -> 71.8 us
  matrix products: 25.9 us -> 0 us
  other arithmetic: 20.2 us -> 2.12 us
  local copies, waits for them, and re-layouts: 24.3 us -> 7.18 us
  blocking collectives: 14.3 us -> 0 us
  between operations: 14.2 us -> 0.68 us
  starting transfers between devices: 7.15 us -> 0 us
    unnamed x2 -> x0, waiting for transfers between devices: 124 us -> none
    pallas_call x0 -> x3, Pallas kernels: none -> 71.8 us  [the longest x1 28.9 us: give_back(): pl.pallas_call(functools.partial(return_kernel, lat_count, lon_count, cap...]
    dot_general x4 -> x0, matrix products: 25.9 us -> none  [the longest x1 9.67 us: shards(): lax.dot_general(misfit, flat_pred, (((0,), (0,)), ((), ())), precision=la...]
    all_to_all x2 -> x0, waiting for transfers between devices: 16.5 us -> none  [the longest x1 16.5 us: route_profiles(): lax.all_to_all(payload, ('lat', 'lon'), split_axis=0, concat_axis=0, tile...]
    all_to_all x1 -> x0, blocking collectives: 14.3 us -> none  [route_ids(): lax.all_to_all(requests, ('lat', 'lon'), split_axis=0, concat_axis=0, til...]
    gather x3 -> x0, local copies, waits for them, and re-layouts: 12.3 us -> none  [the longest x1 4.35 us: shards(): step_rows = increment[wanted]]
    scatter-add x1 -> x0, other arithmetic: 8.4 us -> none  [shards(): jnp.zeros((column_count, profile_len), jnp.float32).at[wanted].add(returned)]
    all_to_all x2 -> x0, starting transfers between devices: 6.89 us -> none  [the longest x1 3.5 us: route_profiles(): lax.all_to_all(payload, ('lat', 'lon'), split_axis=0, concat_axis=0, tile...]
  transfers between devices with their start and end apart: 3 -> 0, of which waited for: 2 -> 0; matrix products, arithmetic and copies ran while one was open for 5% -> 0% of each run, Pallas kernels for 0% -> 0%
where the time goes in v2:
time: 82.5 us; the launch traced here: 81.7 us
  Pallas kernels  71.8 us (87%)
  local copies, waits for them, and re-layouts  7.18 us (9%)
  other arithmetic  2.12 us (3%)
    pallas_call x1, Pallas kernels, give_back(): pl.pallas_call(functools.partial(return_kernel, lat_count, lon_count, cap...  28.9 us
    pallas_call x1, Pallas kernels, fetch(): pl.pallas_call(functools.partial(fetch_kernel, lat_count, lon_count, capa...  26.5 us
    pallas_call x1, Pallas kernels, compute(): pl.pallas_call(functools.partial(compute_kernel, block_len, scaling), gri...  16.4 us
    unnamed x2, local copies, waits for them, and re-layouts  3.39 us
    reshape x2, local copies, waits for them, and re-layouts, shards(): bias.reshape(npredictors, devices, channels // devices).transpose(1, 0, 2)  2.06 us

profile of v2, /device:TPU:0, one launch (start us, length us, event | category | flops | bytes accessed | tf_op | source)
XLA Modules:
  0.0 81.7 jit_solution(17948389629236558404)
XLA Ops:
  0.6 0.1 pad.5.clone
  0.7 0.7 reduce-precision_convert_fusion
  1.4 0.6 maximum_bitcast_fusion.flip_ref
  2.0 1.3 %reshape.27.weight_ref = f32[1,4352]{1,0:T(1,128)} reshape(f32[4352]{0:T(1024)} %param.15) | data formatting | bytes 34816 | tf_op jit(solution)/shard_map/reshape | solution.py:414
  3.4 0.2 copy.15
  3.5 0.2 copy.17
  3.7 0.8 maximum_maximum_fusion.aug_ref
  4.5 26.5 %fetch_profiles.1 = (bf16[512,384]{1,0:T(8,128)(2,1)}, s32[1,512]{1,0:T(1,128)}, s32[1,768]{1,0:T(1,128)}) custom-call(s32[1,512]{1,0:T(1,128)} %bitcast.15, bf16[1024,384]{1,0:T(8,128)(2,1)} %base_ref.3, bf16[1024,384]{1,0:T(8,128)(2,1)} %step_ref.1), custom_call_target="tpu_custom_call" | custom-call | tf_op jit(solution)/shard_map/fetch_profiles/pallas_call | solution.py:179
  31.0 16.4 %operator.1 = (bf16[512,4352]{1,0:T(8,128)(2,1)}, bf16[512,384]{1,0:T(8,128)(2,1)}, f32[8,4352]{1,0:T(8,128)}) custom-call(s32[4]{0:T(128)} %count_ref.1, bf16[512,384]{1,0:T(8,128)(2,1)} %get-tuple-element.11.pred_ref, bf16[512,128]{1,0:T(8,128)(2,1)} %maximum_maximum_fusion.aug_ref, bf16[16,512]{1,0:T(8,128)(2,1)} %maximum_bitcast_fusion.flip_ref, ...), custom_call_target="tpu_custom_call" | custom-call | tf_op jit(solution)/shard_map/operator/pallas_call | solution.py:281
  47.4 1.2 %reshape.29 = f32[8,32,136]{2,1,0:T(8,128)S(1)} reshape(f32[8,4352]{1,0:T(8,128)} %get-tuple-element.16) | data formatting | bytes 278528 | tf_op jit(solution)/shard_map/reshape | solution.py:416
  48.6 0.9 %copy.20 = f32[8,32,136]{2,0,1:T(8,128)} copy(f32[8,32,136]{2,1,0:T(8,128)S(1)} %reshape.29) | data formatting | bytes 278528 | tf_op jit(solution)/shard_map/reshape | solution.py:416
  49.5 28.9 %return_adjoint.1 = (bf16[1024,384]{1,0:T(8,128)(2,1)}, f32[8,136]{1,0:T(8,128)}) custom-call(bf16[512,384]{1,0:T(8,128)(2,1)} %get-tuple-element.13.pulled_ref, s32[1,512]{1,0:T(1,128)} %get-tuple-element.14.position_ref, s32[1,768]{1,0:T(1,128)} %get-tuple-element.15.wanted_ref, f32[32,8,136]{2,1,0:T(8,128)} %bitcast.13, bf16[1024,384]{1,0:T(8,128)(2,1)} %base_ref.3), custom_call_target="tpu_custom_call" | custom-call | tf_op jit(solution)/shard_map/return_adjoint/pallas_call | solution.py:359
  78.4 2.1 %copy.23 = bf16[1024,384]{1,0:T(8,128)(2,1)} copy(bf16[1024,384]{1,0:T(8,128)(2,1)} %get-tuple-element.25) | data formatting | bytes 1572864
  80.4 1.3 %copy.24 = f32[136,8]{0,1:T(8,128)} copy(f32[136,8]{0,1:T(8,128)} %bitcast.14) | data formatting | bytes 8704
  (1 shorter events, 0.0 us)

commit v3 on v2

--- a/solution.py
+++ b/solution.py
@@ -206,8 +206,7 @@
     scaling,
     count_ref,
     pred_ref,
-    aug_ref,
-    flip_ref,
+    side_ref,
     coef_ref,
     dep_ref,
     beta_ref,
@@ -216,7 +215,9 @@
     pulled_ref,
     bias_ref,
     left,
+    flip,
     total,
+    product,
     main,
     rest,
 ):
@@ -227,7 +228,13 @@
     @pl.when(step == 0)
     def _():
         left[:, :profile_len] = pred_ref[...]
-        left[:, profile_len:] = aug_ref[...]
+        side = side_ref[...]
+        side_main = side.astype(jnp.bfloat16).astype(jnp.float32)
+        side_rest = side - side_main
+        flip[...] = jnp.concatenate([side_main, side_rest], axis=0).astype(jnp.bfloat16)
+        blank = jnp.zeros((SPAN - 3 * npredictors, side.shape[1]), jnp.float32)
+        stack = jnp.concatenate([side_main, side_main, side_rest, blank], axis=0)
+        left[:, profile_len:] = stack.T.astype(jnp.bfloat16)
         total[...] = jnp.zeros_like(total)
 
     coef = coef_ref[...]
@@ -238,10 +245,11 @@
     extra = jnp.concatenate([beta_main, beta_rest, beta_main, filler], axis=0)
     right = jnp.concatenate([coef, extra.astype(jnp.bfloat16)], axis=0)
     weight = weight_ref[...]
+    product[...] = dot(left[...], right)
     for block in range(pred_ref.shape[0] // block_len):
         part = pl.ds(block * block_len, block_len)
         present = iota((block_len, tile), 0) < count_ref[block]
-        radiance = jnp.where(present, dot(left[part, :], right), 0.0)
+        radiance = jnp.where(present, product[part, :], 0.0)
         rad_ref[part, :] = radiance.astype(jnp.bfloat16)
         misfit = weight * (radiance - dep_ref[part, :].astype(jnp.float32))
         misfit = jnp.where(present, misfit, 0.0)
@@ -249,8 +257,8 @@
         main[part, :] = misfit_b
         rest[part, :] = (misfit - misfit_b.astype(jnp.float32)).astype(jnp.bfloat16)
     total[...] += dot_nt(main[...], coef)
-    whole = dot(flip_ref[...], main[...])
-    small = dot(flip_ref[...], rest[...])
+    whole = dot(flip[...], main[...])
+    small = dot(flip[...], rest[...])
     bias_ref[...] = scaling * (
         whole[:npredictors] + whole[npredictors:] + small[:npredictors]
     )
@@ -260,18 +268,11 @@
         pulled_ref[...] = total[...].astype(jnp.bfloat16)
 
 
-def compute(block_len, scaling, obs_count, pred, flat_pred, coef, dep, beta, weight):
+def compute(block_len, scaling, obs_count, pred, side, coef, dep, beta, weight):
     slots, profile_len = pred.shape
     channels = coef.shape[1]
-    npredictors = flat_pred.shape[1]
+    npredictors = side.shape[0]
     tile = max(t for t in range(128, 513, 128) if channels % t == 0)
-    main = lax.reduce_precision(flat_pred, 8, 7)
-    rest = (flat_pred - main).astype(jnp.bfloat16)
-    main = main.astype(jnp.bfloat16)
-    filler = jnp.zeros((slots, SPAN - 3 * npredictors), jnp.bfloat16)
-    aug = jnp.concatenate([main, main, rest, filler], axis=1)
-    flip = jnp.concatenate([main, rest], axis=1).T
-
     def fixed(shape):
         return pl.BlockSpec(shape, lambda i: (0, 0))
 
@@ -289,8 +290,7 @@
         in_specs=[
             pl.BlockSpec(memory_space=pltpu.SMEM),
             fixed((slots, profile_len)),
-            fixed((slots, SPAN)),
-            fixed((2 * npredictors, slots)),
+            fixed((npredictors, slots)),
             moving(profile_len),
             moving(slots),
             moving(npredictors),
@@ -299,13 +299,15 @@
         out_specs=(moving(slots), fixed((slots, profile_len)), moving(npredictors)),
         scratch_shapes=[
             pltpu.VMEM((slots, profile_len + SPAN), jnp.bfloat16),
+            pltpu.VMEM((2 * npredictors, slots), jnp.bfloat16),
             pltpu.VMEM((slots, profile_len), jnp.float32),
+            pltpu.VMEM((slots, tile), jnp.float32),
             pltpu.VMEM((slots, tile), jnp.bfloat16),
             pltpu.VMEM((slots, tile), jnp.bfloat16),
         ],
         compiler_params=pltpu.CompilerParams(vmem_limit_bytes=GRANT),
         name="operator",
-    )(obs_count, pred, aug, flip, coef, dep, beta, weight)
+    )(obs_count, pred, side, coef, dep, beta, weight)
 
 
 def return_kernel(
@@ -349,7 +351,7 @@
     arrived = inbound[...].astype(jnp.float32).reshape(rows, profile_len).astype(jnp.bfloat16)
     grad_ref[...] = (dot(collector[...], arrived) * jacobian[...]).astype(jnp.bfloat16)
     wait_all(devices, peer, bias_ref, shares, bias_send, bias_recv)
-    sum_ref[...] = jnp.sum(shares[...], axis=0)
+    sum_ref[...] = jnp.sum(shares[...].astype(jnp.float32), axis=0)
 
 
 def give_back(lat_count, lon_count, capacity, pulled, position, wanted, bias, background):
@@ -367,7 +369,7 @@
         scratch_shapes=[
             pltpu.VMEM((devices, capacity, profile_len), jnp.bfloat16),
             pltpu.VMEM((devices, capacity, profile_len), jnp.bfloat16),
-            pltpu.VMEM(bias.shape, jnp.float32),
+            pltpu.VMEM(bias.shape, bias.dtype),
             pltpu.VMEM((column_count, rows), jnp.bfloat16),
             pltpu.VMEM((column_count, profile_len), jnp.float32),
         ]
@@ -407,13 +409,13 @@
         scaling,
         obs_count,
         pred,
-        bias_pred.reshape(slot_count, npredictors),
+        bias_pred.reshape(slot_count, npredictors).T,
         coefficients,
         departures.reshape(slot_count, channels),
         beta_incr,
         obs_weight.reshape(1, channels),
     )
-    bias = bias.reshape(npredictors, devices, channels // devices).transpose(1, 0, 2)
+    bias = bias.astype(jnp.bfloat16).reshape(npredictors, devices, channels // devices).transpose(1, 0, 2)
     column_grad, bias_grad = give_back(
         lat_count, lon_count, capacity, pulled, position, wanted, bias, background
     )

time: 82.5 us -> 80.1 us (0.971)
  local copies, waits for them, and re-layouts: 7.18 us -> 5.82 us
  other arithmetic: 2.12 us -> 0.92 us
    pallas_call x1, Pallas kernels: 16.4 us -> 18.1 us  [compute(): pl.pallas_call(functools.partial(compute_kernel, block_len, scaling), gri...]
    pallas_call x1, Pallas kernels: 28.9 us -> 27.4 us  [give_back(): pl.pallas_call(functools.partial(return_kernel, lat_count, lon_count, cap...]
    reshape x2, local copies, waits for them, and re-layouts: 2.06 us -> 1.1 us  [shards(): bias.astype(jnp.bfloat16).reshape(npredictors, devices, channels // devices)]
where the time goes in v3:
time: 80.1 us; the launch traced here: 79.4 us
  Pallas kernels  72 us (90%)
  local copies, waits for them, and re-layouts  5.82 us (7%)
  other arithmetic  0.92 us (1%)
    pallas_call x1, Pallas kernels, give_back(): pl.pallas_call(functools.partial(return_kernel, lat_count, lon_count, cap...  27.4 us
    pallas_call x1, Pallas kernels, fetch(): pl.pallas_call(functools.partial(fetch_kernel, lat_count, lon_count, capa...  26.5 us
    pallas_call x1, Pallas kernels, compute(): pl.pallas_call(functools.partial(compute_kernel, block_len, scaling), gri...  18.1 us
    unnamed x2, local copies, waits for them, and re-layouts  3.39 us

profile of v3, /device:TPU:0, one launch (start us, length us, event | category | flops | bytes accessed | tf_op | source)
XLA Modules:
  0.0 79.4 jit_solution(12098024586444514104)
XLA Ops:
  0.6 1.3 %reshape.27.weight_ref = f32[1,4352]{1,0:T(1,128)} reshape(f32[4352]{0:T(1024)} %param.15) | data formatting | bytes 34816 | tf_op jit(solution)/shard_map/reshape | solution.py:416
  2.0 26.5 %fetch_profiles.1 = (bf16[512,384]{1,0:T(8,128)(2,1)}, s32[1,512]{1,0:T(1,128)}, s32[1,768]{1,0:T(1,128)}) custom-call(s32[1,512]{1,0:T(1,128)} %bitcast.14, bf16[1024,384]{1,0:T(8,128)(2,1)} %base_ref.3, bf16[1024,384]{1,0:T(8,128)(2,1)} %step_ref.1), custom_call_target="tpu_custom_call" | custom-call | tf_op jit(solution)/shard_map/fetch_profiles/pallas_call | solution.py:179
  28.5 18.1 %operator.1 = (bf16[512,4352]{1,0:T(8,128)(2,1)}, bf16[512,384]{1,0:T(8,128)(2,1)}, f32[8,4352]{1,0:T(8,128)}) custom-call(s32[4]{0:T(128)} %count_ref.1, bf16[512,384]{1,0:T(8,128)(2,1)} %get-tuple-element.11.pred_ref, f32[8,512]{1,0:T(8,128)} %bitcast.12, bf16[384,4352]{1,0:T(8,128)(2,1)} %coef_ref.1, bf16[512,4352]{1,0:T(8,128)(2,1)} %bitcast.10, ...), custom_call_target="tpu_custom_call" | custom-call | tf_op jit(solution)/shard_map/operator/pallas_call | solution.py:282
  46.6 0.9 %convert_element_type.3 = bf16[8,4352]{1,0:T(8,128)(2,1)S(1)} convert(f32[8,4352]{1,0:T(8,128)} %get-tuple-element.16) | non-fusion elementwise | flops 34816 | bytes 208896 | tf_op jit(solution)/shard_map/convert_element_type | solution.py:418
  47.5 0.4 reshape.29
  47.9 0.7 copy.14
  48.6 27.4 %return_adjoint.1 = (bf16[1024,384]{1,0:T(8,128)(2,1)}, f32[8,136]{1,0:T(8,128)}) custom-call(bf16[512,384]{1,0:T(8,128)(2,1)} %get-tuple-element.13.pulled_ref, s32[1,512]{1,0:T(1,128)} %get-tuple-element.14.position_ref, s32[1,768]{1,0:T(1,128)} %get-tuple-element.15.wanted_ref, bf16[32,8,136]{2,1,0:T(8,128)(2,1)} %bitcast.11, bf16[1024,384]{1,0:T(8,128)(2,1)} %base_ref.3), custom_call_target="tpu_custom_call" | custom-call | tf_op jit(solution)/shard_map/return_adjoint/pallas_call | solution.py:361
  76.0 2.1 %copy.17 = bf16[1024,384]{1,0:T(8,128)(2,1)} copy(bf16[1024,384]{1,0:T(8,128)(2,1)} %get-tuple-element.23) | data formatting | bytes 1572864
  78.1 1.3 %copy.18 = f32[136,8]{0,1:T(8,128)} copy(f32[136,8]{0,1:T(8,128)} %bitcast.13) | data formatting | bytes 8704

commit v4 on v3

--- a/solution.py
+++ b/solution.py
@@ -1,4 +1,5 @@
 import functools
+import math
 
 import jax
 import jax.numpy as jnp
@@ -16,9 +17,10 @@
 def peers_of(lat_count, lon_count):
     devices = lat_count * lon_count
     me = lax.axis_index("lat") * lon_count + lax.axis_index("lon")
+    stride = next(s for s in range(lon_count + 3, devices + lon_count + 4) if math.gcd(s, devices) == 1)
 
     def peer(offset):
-        other = lax.rem(me + offset, devices)
+        other = lax.rem(me + offset * stride, devices)
         return other, (lax.div(other, lon_count), lax.rem(other, lon_count))
 
     return me, peer
@@ -217,7 +219,6 @@
     left,
     flip,
     total,
-    product,
     main,
     rest,
 ):
@@ -245,11 +246,10 @@
     extra = jnp.concatenate([beta_main, beta_rest, beta_main, filler], axis=0)
     right = jnp.concatenate([coef, extra.astype(jnp.bfloat16)], axis=0)
     weight = weight_ref[...]
-    product[...] = dot(left[...], right)
     for block in range(pred_ref.shape[0] // block_len):
         part = pl.ds(block * block_len, block_len)
         present = iota((block_len, tile), 0) < count_ref[block]
-        radiance = jnp.where(present, product[part, :], 0.0)
+        radiance = jnp.where(present, dot(left[part, :], right), 0.0)
         rad_ref[part, :] = radiance.astype(jnp.bfloat16)
         misfit = weight * (radiance - dep_ref[part, :].astype(jnp.float32))
         misfit = jnp.where(present, misfit, 0.0)
@@ -259,9 +259,8 @@
     total[...] += dot_nt(main[...], coef)
     whole = dot(flip[...], main[...])
     small = dot(flip[...], rest[...])
-    bias_ref[...] = scaling * (
-        whole[:npredictors] + whole[npredictors:] + small[:npredictors]
-    )
+    share = whole[:npredictors] + whole[npredictors:] + small[:npredictors]
+    bias_ref[...] = (scaling * share).astype(bias_ref.dtype)
 
     @pl.when(step == pl.num_programs(0) - 1)
     def _():
@@ -285,7 +284,7 @@
         out_shape=(
             jax.ShapeDtypeStruct((slots, channels), jnp.bfloat16),
             jax.ShapeDtypeStruct((slots, profile_len), jnp.bfloat16),
-            jax.ShapeDtypeStruct((npredictors, channels), jnp.float32),
+            jax.ShapeDtypeStruct((npredictors, channels), jnp.bfloat16),
         ),
         in_specs=[
             pl.BlockSpec(memory_space=pltpu.SMEM),
@@ -301,7 +300,6 @@
             pltpu.VMEM((slots, profile_len + SPAN), jnp.bfloat16),
             pltpu.VMEM((2 * npredictors, slots), jnp.bfloat16),
             pltpu.VMEM((slots, profile_len), jnp.float32),
-            pltpu.VMEM((slots, tile), jnp.float32),
             pltpu.VMEM((slots, tile), jnp.bfloat16),
             pltpu.VMEM((slots, tile), jnp.bfloat16),
         ],
@@ -415,7 +413,7 @@
         beta_incr,
         obs_weight.reshape(1, channels),
     )
-    bias = bias.astype(jnp.bfloat16).reshape(npredictors, devices, channels // devices).transpose(1, 0, 2)
+    bias = bias.reshape(npredictors, devices, channels // devices).transpose(1, 0, 2)
     column_grad, bias_grad = give_back(
         lat_count, lon_count, capacity, pulled, position, wanted, bias, background
     )

time: 80.1 us -> 81.1 us (1.012)
  Pallas kernels: 72 us -> 73 us
  other arithmetic: 0.92 us -> 0 us
  local copies, waits for them, and re-layouts: 5.82 us -> 6.7 us
    pallas_call x1, Pallas kernels: 26.5 us -> 31.8 us  [fetch(): pl.pallas_call(functools.partial(fetch_kernel, lat_count, lon_count, capa...]
    pallas_call x1, Pallas kernels: 27.4 us -> 24.9 us  [give_back(): pl.pallas_call(functools.partial(return_kernel, lat_count, lon_count, cap...]
    pallas_call x1, Pallas kernels: 18.1 us -> 16.3 us  [compute(): pl.pallas_call(functools.partial(compute_kernel, block_len, scaling), gri...]
    convert_element_type x1 -> x0, other arithmetic: 0.92 us -> none  [shards(): bias.astype(jnp.bfloat16).reshape(npredictors, devices, channels // devices)]
    reshape x2, local copies, waits for them, and re-layouts: 1.1 us -> 1.98 us  [shards(): bias.reshape(npredictors, devices, channels // devices).transpose(1, 0, 2)]
where the time goes in v4:
time: 81.1 us; the launch traced here: 80.4 us
  Pallas kernels  73 us (90%)
  local copies, waits for them, and re-layouts  6.7 us (8%)
    pallas_call x1, Pallas kernels, fetch(): pl.pallas_call(functools.partial(fetch_kernel, lat_count, lon_count, capa...  31.8 us
    pallas_call x1, Pallas kernels, give_back(): pl.pallas_call(functools.partial(return_kernel, lat_count, lon_count, cap...  24.9 us
    pallas_call x1, Pallas kernels, compute(): pl.pallas_call(functools.partial(compute_kernel, block_len, scaling), gri...  16.3 us
    unnamed x2, local copies, waits for them, and re-layouts  3.39 us
    reshape x2, local copies, waits for them, and re-layouts, shards(): bias.reshape(npredictors, devices, channels // devices).transpose(1, 0, 2)  1.98 us

profile of v4, /device:TPU:0, one launch (start us, length us, event | category | flops | bytes accessed | tf_op | source)
XLA Modules:
  0.0 80.4 jit_solution(17471757735445904132)
XLA Ops:
  0.6 1.3 %reshape.27.weight_ref = f32[1,4352]{1,0:T(1,128)} reshape(f32[4352]{0:T(1024)} %param.15) | data formatting | bytes 34816 | tf_op jit(solution)/shard_map/reshape | solution.py:414
  2.0 31.8 %fetch_profiles.1 = (bf16[512,384]{1,0:T(8,128)(2,1)}, s32[1,512]{1,0:T(1,128)}, s32[1,768]{1,0:T(1,128)}) custom-call(s32[1,512]{1,0:T(1,128)} %bitcast.14, bf16[1024,384]{1,0:T(8,128)(2,1)} %base_ref.3, bf16[1024,384]{1,0:T(8,128)(2,1)} %step_ref.1), custom_call_target="tpu_custom_call" | custom-call | tf_op jit(solution)/shard_map/fetch_profiles/pallas_call | solution.py:181
  33.8 16.3 %operator.1 = (bf16[512,4352]{1,0:T(8,128)(2,1)}, bf16[512,384]{1,0:T(8,128)(2,1)}, bf16[8,4352]{1,0:T(8,128)(2,1)}) custom-call(s32[4]{0:T(128)} %count_ref.1, bf16[512,384]{1,0:T(8,128)(2,1)} %get-tuple-element.11.pred_ref, f32[8,512]{1,0:T(8,128)} %bitcast.12, bf16[384,4352]{1,0:T(8,128)(2,1)} %coef_ref.1, bf16[512,4352]{1,0:T(8,128)(2,1)} %bitcast.10, ...), custom_call_target="tpu_custom_call" | custom-call | tf_op jit(solution)/shard_map/operator/pallas_call | solution.py:281
  50.1 1.3 %reshape.29 = bf16[8,32,136]{2,1,0:T(8,128)(2,1)S(1)} reshape(bf16[8,4352]{1,0:T(8,128)(2,1)} %get-tuple-element.16) | data formatting | bytes 139264 | tf_op jit(solution)/shard_map/reshape | solution.py:416
  51.3 0.7 copy.14
  52.1 24.9 %return_adjoint.1 = (bf16[1024,384]{1,0:T(8,128)(2,1)}, f32[8,136]{1,0:T(8,128)}) custom-call(bf16[512,384]{1,0:T(8,128)(2,1)} %get-tuple-element.13.pulled_ref, s32[1,512]{1,0:T(1,128)} %get-tuple-element.14.position_ref, s32[1,768]{1,0:T(1,128)} %get-tuple-element.15.wanted_ref, bf16[32,8,136]{2,1,0:T(8,128)(2,1)} %bitcast.11, bf16[1024,384]{1,0:T(8,128)(2,1)} %base_ref.3), custom_call_target="tpu_custom_call" | custom-call | tf_op jit(solution)/shard_map/return_adjoint/pallas_call | solution.py:359
  77.0 2.1 %copy.17 = bf16[1024,384]{1,0:T(8,128)(2,1)} copy(bf16[1024,384]{1,0:T(8,128)(2,1)} %get-tuple-element.23) | data formatting | bytes 1572864
  79.1 1.3 %copy.18 = f32[136,8]{0,1:T(8,128)} copy(f32[136,8]{0,1:T(8,128)} %bitcast.13) | data formatting | bytes 8704

commit v5 on v4

--- a/solution.py
+++ b/solution.py
@@ -1,5 +1,4 @@
 import functools
-import math
 
 import jax
 import jax.numpy as jnp
@@ -17,10 +16,9 @@
 def peers_of(lat_count, lon_count):
     devices = lat_count * lon_count
     me = lax.axis_index("lat") * lon_count + lax.axis_index("lon")
-    stride = next(s for s in range(lon_count + 3, devices + lon_count + 4) if math.gcd(s, devices) == 1)
 
     def peer(offset):
-        other = lax.rem(me + offset * stride, devices)
+        other = lax.rem(me + offset, devices)
         return other, (lax.div(other, lon_count), lax.rem(other, lon_count))
 
     return me, peer

time: 81.1 us -> 78.3 us (0.965)
  Pallas kernels: 73 us -> 70.2 us
    pallas_call x1, Pallas kernels: 31.8 us -> 26.5 us  [fetch(): pl.pallas_call(functools.partial(fetch_kernel, lat_count, lon_count, capa...]
    pallas_call x1, Pallas kernels: 24.9 us -> 27.4 us  [give_back(): pl.pallas_call(functools.partial(return_kernel, lat_count, lon_count, cap...]
where the time goes in v5:
time: 78.3 us; the launch traced here: 77.6 us
  Pallas kernels  70.2 us (90%)
  local copies, waits for them, and re-layouts  6.7 us (9%)
    pallas_call x1, Pallas kernels, give_back(): pl.pallas_call(functools.partial(return_kernel, lat_count, lon_count, cap...  27.4 us
    pallas_call x1, Pallas kernels, fetch(): pl.pallas_call(functools.partial(fetch_kernel, lat_count, lon_count, capa...  26.5 us
    pallas_call x1, Pallas kernels, compute(): pl.pallas_call(functools.partial(compute_kernel, block_len, scaling), gri...  16.3 us
    unnamed x2, local copies, waits for them, and re-layouts  3.39 us
    reshape x2, local copies, waits for them, and re-layouts, shards(): bias.reshape(npredictors, devices, channels // devices).transpose(1, 0, 2)  1.98 us

profile of v5, /device:TPU:0, one launch (start us, length us, event | category | flops | bytes accessed | tf_op | source)
XLA Modules:
  0.0 77.6 jit_solution(9252301337931361999)
XLA Ops:
  0.6 1.3 %reshape.27.weight_ref = f32[1,4352]{1,0:T(1,128)} reshape(f32[4352]{0:T(1024)} %param.15) | data formatting | bytes 34816 | tf_op jit(solution)/shard_map/reshape | solution.py:412
  2.0 26.5 %fetch_profiles.1 = (bf16[512,384]{1,0:T(8,128)(2,1)}, s32[1,512]{1,0:T(1,128)}, s32[1,768]{1,0:T(1,128)}) custom-call(s32[1,512]{1,0:T(1,128)} %bitcast.14, bf16[1024,384]{1,0:T(8,128)(2,1)} %base_ref.3, bf16[1024,384]{1,0:T(8,128)(2,1)} %step_ref.1), custom_call_target="tpu_custom_call" | custom-call | tf_op jit(solution)/shard_map/fetch_profiles/pallas_call | solution.py:179
  28.5 16.3 %operator.1 = (bf16[512,4352]{1,0:T(8,128)(2,1)}, bf16[512,384]{1,0:T(8,128)(2,1)}, bf16[8,4352]{1,0:T(8,128)(2,1)}) custom-call(s32[4]{0:T(128)} %count_ref.1, bf16[512,384]{1,0:T(8,128)(2,1)} %get-tuple-element.11.pred_ref, f32[8,512]{1,0:T(8,128)} %bitcast.12, bf16[384,4352]{1,0:T(8,128)(2,1)} %coef_ref.1, bf16[512,4352]{1,0:T(8,128)(2,1)} %bitcast.10, ...), custom_call_target="tpu_custom_call" | custom-call | tf_op jit(solution)/shard_map/operator/pallas_call | solution.py:279
  44.8 1.3 %reshape.29 = bf16[8,32,136]{2,1,0:T(8,128)(2,1)S(1)} reshape(bf16[8,4352]{1,0:T(8,128)(2,1)} %get-tuple-element.16) | data formatting | bytes 139264 | tf_op jit(solution)/shard_map/reshape | solution.py:414
  46.0 0.7 copy.14
  46.8 27.4 %return_adjoint.1 = (bf16[1024,384]{1,0:T(8,128)(2,1)}, f32[8,136]{1,0:T(8,128)}) custom-call(bf16[512,384]{1,0:T(8,128)(2,1)} %get-tuple-element.13.pulled_ref, s32[1,512]{1,0:T(1,128)} %get-tuple-element.14.position_ref, s32[1,768]{1,0:T(1,128)} %get-tuple-element.15.wanted_ref, bf16[32,8,136]{2,1,0:T(8,128)(2,1)} %bitcast.11, bf16[1024,384]{1,0:T(8,128)(2,1)} %base_ref.3), custom_call_target="tpu_custom_call" | custom-call | tf_op jit(solution)/shard_map/return_adjoint/pallas_call | solution.py:357
  74.2 2.1 %copy.17 = bf16[1024,384]{1,0:T(8,128)(2,1)} copy(bf16[1024,384]{1,0:T(8,128)(2,1)} %get-tuple-element.23) | data formatting | bytes 1572864
  76.3 1.3 %copy.18 = f32[136,8]{0,1:T(8,128)} copy(f32[136,8]{0,1:T(8,128)} %bitcast.13) | data formatting | bytes 8704
